TPU v7x, 32 devices: a whole 2x2x4 slice. The times are simulated.
32 devices in a mesh: seq: 4 (over y, core), vocab: 8 (over z, x).
Axes of the slice: x: 2, y: 2, z: 4, core: 2. Of those that a mesh axis runs over, the one named last changes fastest.
Arguments:
- hidden: bfloat16 [2, 512, 5120], P(None, 'seq'), may hold values from -128 to 128
- head_weight: bfloat16 [5120, 77824], P('seq', 'vocab'), may hold values from -1 to 1
- ref_logits: bfloat16 [2, 512, 77824], P(None, 'seq', 'vocab'), may hold values from -320 to 320
- token_ids: int32 [2, 512], P(None, 'seq'), may hold values from 0 to 77823
- end_pos: int32 [2], replicated, may hold values from 256 to 511
- loss_mask: int32 [2, 512], P(None, 'seq'), may hold values 0 or 1
- scores: float32 [2], replicated, may hold values from -8 to 8
Outputs:
- logit_grad: bfloat16 [2, 512, 77824], P(None, 'seq', 'vocab')
- hidden_grad: bfloat16 [2, 512, 5120], P(None, 'seq', 'vocab')
- advantages: float32 [2, 512], P(None, 'seq')
All inputs are finite; a program needn't handle non-finite values. No bound on the sum of `loss_mask` on one device may be relied on, other than what follows from the above.
Results may differ from a plain program's by a relative error of at most 0.0039.
The roundings to bfloat16 on the way count: a program that leaves them out, or rounds other values in their place, can miss the bound.
Values may be sent and summed in bfloat16 or wider, within the bound.
A program may use at most 128 MiB of HBM per device.

v0:
```python
import jax
import jax.numpy as jnp
from jax import lax
from jax.sharding import PartitionSpec as P


def from_behind(shard, axis, by):
    devices = lax.axis_size(axis)
    pairs = [(i, i + by) for i in range(devices) if 0 <= i + by < devices]
    return lax.ppermute(shard, axis, pairs)


def per_device(hidden, head_weight, ref_logits, token_ids, end_pos, loss_mask, scores):
    batch, segment, width = hidden.shape
    vocab_dev = head_weight.shape[1]
    seq_start = lax.axis_index("seq") * segment
    vocab_start = lax.axis_index("vocab") * vocab_dev
    split_hidden = lax.all_to_all(hidden, "seq", split_axis=2, concat_axis=1, tiled=True)
    logits = jnp.transpose(
        lax.psum_scatter(
            jnp.einsum(
                "bsd,dv->sbv", split_hidden, head_weight, preferred_element_type=jnp.float32
            ),
            "seq",
            scatter_dimension=0,
            tiled=True,
        ),
        (1, 0, 2),
    )
    refs = ref_logits.astype(jnp.float32)
    local_top = jnp.max(logits, axis=2)
    local_rtop = jnp.max(refs, axis=2)
    top_policy, top_ref = lax.pmax((local_top, local_rtop), "vocab")
    expo = jnp.exp(logits - top_policy[:, :, None])
    total, ref_total, weighted = lax.psum(
        (
            jnp.sum(expo, axis=2),
            jnp.sum(jnp.exp(refs - top_ref[:, :, None]), axis=2),
            jnp.sum(expo * (logits - refs), axis=2),
        ),
        "vocab",
    )
    lse_policy = top_policy + jnp.log(total)
    lse_ref = top_ref + jnp.log(ref_total)
    kl_value = weighted / total - lse_policy + lse_ref
    position = seq_start + lax.broadcasted_iota(jnp.int32, (1, segment), 1)
    live = ((loss_mask == 1) & (position <= end_pos[:, None])).astype(jnp.float32)
    at_end = (position == end_pos[:, None]).astype(jnp.float32)
    reward = -0.01 * kl_value * live + scores[:, None] * at_end
    upper = (
        lax.broadcasted_iota(jnp.int32, (segment, segment), 0)
        >= lax.broadcasted_iota(jnp.int32, (segment, segment), 1)
    ).astype(jnp.float32)
    local_returns = jnp.dot(reward, upper, precision=lax.Precision.HIGHEST)
    totals = jnp.sum(reward, axis=1)
    carried = jnp.zeros_like(totals)
    for _ in range(lax.axis_size("seq") - 1):
        carried = from_behind(totals + carried, "seq", -1)
    returns = local_returns + carried[:, None]
    count, first_moment, second_moment = lax.psum(
        (jnp.sum(live), jnp.sum(live * returns), jnp.sum(live * returns * returns)), "seq"
    )
    count = jnp.maximum(count, 1.0)
    mean = first_moment / count
    var = second_moment / count - mean * mean
    advantages = (returns - mean) / jnp.sqrt(var + 1e-05)
    factor = live * advantages / count
    prob = jnp.exp(logits - lse_policy[:, :, None])
    column = vocab_start + lax.broadcasted_iota(jnp.int32, (1, 1, vocab_dev), 2)
    onehot = (column == token_ids[:, :, None]).astype(jnp.float32)
    logit_grad = (factor[:, :, None] * (prob - onehot)).astype(jnp.bfloat16)
    all_grads = lax.all_gather(logit_grad, "seq", axis=1, tiled=True)
    slice_grad = jnp.einsum(
        "bsv,dv->bsd", all_grads, head_weight, preferred_element_type=jnp.float32
    )
    partial_grad = lax.all_to_all(slice_grad, "seq", split_axis=1, concat_axis=2, tiled=True)
    hidden_grad = lax.psum_scatter(partial_grad, "vocab", scatter_dimension=2, tiled=True).astype(
        jnp.bfloat16
    )
    return (logit_grad, hidden_grad, advantages)


def solution(mesh):
    in_specs = (
        P(None, "seq", None),
        P("seq", "vocab"),
        P(None, "seq", "vocab"),
        P(None, "seq"),
        P(),
        P(None, "seq"),
        P(),
    )
    out_specs = (P(None, "seq", "vocab"), P(None, "seq", "vocab"), P(None, "seq"))
    return jax.shard_map(
        per_device, mesh=mesh, in_specs=in_specs, out_specs=out_specs, check_vma=False
    )
```

profile of v0, /device:TPU:0, one launch (start us, length us, event | category | flops | bytes accessed | tf_op | source)
XLA Modules:
  0.0 799.1 jit_solution(6188763925158385231)
XLA Ops:
  7.2 0.0 reduce-scatter.3.cloned.1.call-start
  7.2 7.4 copy.16
  14.6 35.6 %all_to_all.36 = bf16[2,128,5120]{1,0,2:T(2,128)(2,1)S(1)} all-to-all(bf16[2,128,5120]{1,0,2:T(2,128)(2,1)} %copy.16), channel_id=1, replica_groups=mesh['seq'=4,'vocab'=8] {'seq'}, dimensions={2} | all-to-all | bytes 5242880 | tf_op jit(solution)/shard_map/all_to_all | solution.py:18
  50.2 4.6 copy.17
  54.9 34.2 %fusion.4 = f32[512,2,9728]{0,2,1:T(8,128)} fusion(bf16[2,512,1280]{2,1,0:T(8,128)(2,1)} %bitcast.41, bf16[1280,9728]{1,0:T(8,128)(2,1)} %param.8), kind=kOutput, calls=%fused_computation.4 | convolution fusion | flops 25501368320 | bytes 67371008 | tf_op jit(solution)/shard_map/bsd,dv->sbv/dot_general | solution.py:21
  89.1 0.0 reduce-scatter.3.cloned.1.call-update
  89.1 0.0 all-gather.2.cloned.1.call-start
  89.1 8.0 copy.19
  97.1 4.5 reduce_max.24
  101.6 258.7 %reduce-scatter.3.cloned.1.call-done = f32[128,2,9728]{0,2,1:T(8,128)} async-done(((f32[512,2,9728]{0,2,1:T(8,128)}), f32[128,2,9728]{0,2,1:T(8,128)}) %reduce-scatter.3.cloned.1.call-update) | async-done | bytes 9961488 | tf_op jit(solution)/shard_map/reduce_scatter | solution.py:20
  360.3 4.6 bitcast_reduce_fusion
  364.9 0.0 copy-start
  364.9 0.0 copy-start.2
  364.9 0.0 copy-start.3
  364.9 0.0 copy-start.1
  364.9 21.3 %all-reduce.1 = (f32[2,128]{1,0:T(2,128)S(1)}, f32[2,128]{1,0:T(2,128)S(1)}) all-reduce(f32[2,128]{1,0:T(2,128)S(1)} %bitcast_reduce_fusion, bf16[2,128]{1,0:T(2,128)(2,1)S(1)} %reduce_max.24), channel_id=1, replica_groups=mesh['seq'=4,'vocab'=8] {'vocab'}, use_global_device_ids=true, to_apply=%region_2.0 | all-reduce | flops 512 | bytes 3584 | tf_op jit(solution)/shard_map/pmax | solution.py:33
  386.3 7.5 fusion.8
  393.8 17.1 %all-reduce = (f32[2,128]{1,0:T(2,128)S(1)}, f32[2,128]{1,0:T(2,128)S(1)}, f32[2,128]{1,0:T(2,128)S(1)}) all-reduce(f32[2,128]{1,0:T(2,128)S(1)} %get-tuple-element.10, f32[2,128]{1,0:T(2,128)S(1)} %get-tuple-element.11, f32[2,128]{1,0:T(2,128)S(1)} %get-tuple-element.9), channel_id=1, replica_groups=mesh['seq'=4,'vocab'=8] {'vocab'}, use_global_device_ids=true, to_apply=%region_6.0 | all-reduce | flops 768 | bytes 6144 | tf_op jit(solution)/shard_map/psum | solution.py:35
  411.0 0.0 copy-done
  411.0 0.0 copy-done.2
  411.0 0.0 copy-done.3
  411.0 0.2 fusion.20
  411.2 1.3 collective-permute-start
  412.5 1.8 collective-permute-done
  414.2 1.3 collective-permute-start.1
  415.5 2.0 collective-permute-done.1
  417.6 1.3 collective-permute-start.2
  418.8 3.6 collective-permute-done.2
  422.4 0.8 select_reduce_fusion
  423.2 8.8 %all-reduce.2 = (f32[]{:T(128)}, f32[]{:T(128)}, f32[]{:T(128)}) all-reduce(f32[]{:T(128)} %get-tuple-element.13, f32[]{:T(128)} %get-tuple-element.14, f32[]{:T(128)} %get-tuple-element.12), channel_id=1, replica_groups=mesh['seq'=4,'vocab'=8] {'seq'}, use_global_device_ids=true, to_apply=%region_17.0 | all-reduce | flops 3 | bytes 24 | tf_op jit(solution)/shard_map/psum | solution.py:60
  434.0 0.6 select_divide_fusion
  434.6 0.0 copy-done.1
  434.6 9.3 %fusion.16 = bf16[2,128,9728]{1,2,0:T(8,128)(2,1)} fusion(f32[128,2,9728]{0,2,1:T(8,128)} %reduce-scatter.3.cloned.1.call-done, s32[2,128]{1,0:T(2,128)S(1)} %copy-done.1, f32[2,128]{1,0:T(2,128)S(1)} %get-tuple-element.28, f32[2,128]{1,0:T(2,128)S(1)} %get-tuple-element.23, s32[9728]{0:T(1024)S(1)} %iota_add_fusion), kind=kLoop, calls=%fused_computation.19 | loop fusion | flops 14942208 | bytes 14984192 | tf_op jit(solution)/shard_map/convert_element_type | solution.py:71
  443.9 0.0 all-gather.2.cloned.1.call-update
  444.0 0.0 reduce-scatter.5.cloned.1.call-start
  444.0 127.4 %all-gather.2.cloned.1.call-done = bf16[2,512,9728]{1,2,0:T(8,128)(2,1)} async-done(((bf16[2,128,9728]{1,2,0:T(8,128)(2,1)}), bf16[2,512,9728]{1,2,0:T(8,128)(2,1)}) %all-gather.2.cloned.1.call-update) | async-done | bytes 19922960 | tf_op jit(solution)/shard_map/all_gather | solution.py:72
  571.4 34.7 %fusion = f32[2,512,1280]{2,1,0:T(8,128)} fusion(bf16[2,512,9728]{1,2,0:T(8,128)(2,1)} %all-gather.2.cloned.1.call-done, bf16[1280,9728]{1,0:T(8,128)(2,1)} %param.8), kind=kOutput, calls=%fused_computation | convolution fusion | flops 25501368320 | bytes 50069504 | tf_op jit(solution)/shard_map/bsv,dv->bsd/dot_general | solution.py:73
  606.1 6.5 copy.21
  612.7 62.0 %all_to_all.37 = f32[2,512,1280]{2,0,1:T(2,128)S(1)} all-to-all(f32[2,512,1280]{2,0,1:T(2,128)S(1)} %copy.21), channel_id=1, replica_groups=mesh['seq'=4,'vocab'=8] {'seq'}, dimensions={1} | all-to-all | bytes 10485760 | tf_op jit(solution)/shard_map/all_to_all | solution.py:76
  674.7 5.7 copy.22
  680.4 7.2 all_to_all.33
  687.6 0.0 reduce-scatter.5.cloned.1.call-update
  687.6 7.9 copy.23
  695.5 95.3 %reduce-scatter.5.cloned.1.call-done = f32[2,128,640]{2,1,0:T(8,128)} async-done(((f32[2,128,5120]{2,1,0:T(8,128)}), f32[2,128,640]{2,1,0:T(8,128)}) %reduce-scatter.5.cloned.1.call-update) | async-done | bytes 655376 | tf_op jit(solution)/shard_map/reduce_scatter | solution.py:77
  790.8 1.8 convert_element_type.21
  (4 shorter events, 0.0 us)
Async XLA Ops:
  7.2 353.2 %reduce-scatter.3.cloned.1.call-start = ((), (), s32[]{:S(2)}) async-start(), calls=%async_computation.4 | async-start | bytes 49807360 | tf_op jit(solution)/shard_map/reduce_scatter | solution.py:20
  89.1 482.3 %all-gather.2.cloned.1.call-start = ((), (), s32[]{:S(2)}) async-start(), calls=%async_computation.5 | async-start | bytes 24903680 | tf_op jit(solution)/shard_map/all_gather | solution.py:72
  364.9 46.1 %copy-start = (s32[2,128]{1,0:T(2,128)S(1)}, s32[2,128]{1,0:T(2,128)}, u32[]{:S(2)}) copy-start(s32[2,128]{1,0:T(2,128)} %param.12) | copy-start | bytes 3076
  364.9 46.1 %copy-start.2 = (f32[2]{0:T(128)S(1)}, f32[2]{0:T(128)}, u32[]{:S(2)}) copy-start(f32[2]{0:T(128)} %param.13) | copy-start | bytes 28
  364.9 46.1 %copy-start.3 = (s32[2]{0:T(128)S(1)}, s32[2]{0:T(128)}, u32[]{:S(2)}) copy-start(s32[2]{0:T(128)} %param.11) | copy-start | bytes 28
  364.9 69.7 %copy-start.1 = (s32[2,128]{1,0:T(2,128)S(1)}, s32[2,128]{1,0:T(2,128)}, u32[]{:S(2)}) copy-start(s32[2,128]{1,0:T(2,128)} %param.10) | copy-start | bytes 3076
  411.2 3.0 collective-permute-start
  414.2 3.3 collective-permute-start.1
  417.6 4.9 collective-permute-start.2
  444.0 346.8 %reduce-scatter.5.cloned.1.call-start = ((), (), s32[]{:S(2)}) async-start(), calls=%async_computation.6 | async-start | bytes 5898240 | tf_op jit(solution)/shard_map/reduce_scatter | solution.py:77
Sparse Core Ops, SparseCore 0:
  89.2 271.0 reduce-scatter.2
  444.1 127.2 all-gather.1
  687.7 102.9 reduce-scatter.4
where the time goes:
time: 800 us; the launch traced here: 799 us
  waiting for transfers between devices  489 us (61%)
  blocking collectives  145 us (18%)
  matrix products  69.7 us (9%)
  local copies, waits for them, and re-layouts  47.4 us (6%)
  other arithmetic  28.6 us (4%)
  between operations  15.8 us (2%)
    reduce_scatter x1, waiting for transfers between devices, per_device(): lax.psum_scatter(jnp.einsum('bsd,dv->sbv', split_hidden, head_weight, pre...  259 us
    all_gather x1, waiting for transfers between devices, per_device(): all_grads = lax.all_gather(logit_grad, 'seq', axis=1, tiled=True)  127 us
    reduce_scatter x1, waiting for transfers between devices, per_device(): lax.psum_scatter(partial_grad, 'vocab', scatter_dimension=2, tiled=True)  95.3 us
    all_to_all x1, blocking collectives, per_device(): lax.all_to_all(slice_grad, 'seq', split_axis=1, concat_axis=2, tiled=True)  62 us
    all_to_all x1, blocking collectives, per_device(): lax.all_to_all(hidden, 'seq', split_axis=2, concat_axis=1, tiled=True)  35.6 us
    dot_general x1, matrix products, per_device(): jnp.einsum('bsv,dv->bsd', all_grads, head_weight, preferred_element_type=...  34.7 us
    dot_general x1, matrix products, per_device(): jnp.einsum('bsd,dv->sbv', split_hidden, head_weight, preferred_element_ty...  34.2 us
    unnamed x11, local copies, waits for them, and re-layouts  23.3 us
  transfers between devices with their start and end apart: 6, of which 6 were waited for; matrix products, arithmetic and copies ran while one was open for 3% of the time, Pallas kernels for 0%

commit v1 on v0

--- a/solution.py
+++ b/solution.py
@@ -73,7 +73,10 @@
     slice_grad = jnp.einsum(
         "bsv,dv->bsd", all_grads, head_weight, preferred_element_type=jnp.float32
     )
-    partial_grad = lax.all_to_all(slice_grad, "seq", split_axis=1, concat_axis=2, tiled=True)
+    partial_grad = jnp.concatenate(
+        lax.all_to_all(jnp.stack(jnp.split(slice_grad, lax.axis_size("seq"), axis=1)), "seq", 0, 0),
+        axis=2,
+    )
     hidden_grad = lax.psum_scatter(partial_grad, "vocab", scatter_dimension=2, tiled=True).astype(
         jnp.bfloat16
     )

time: 800 us -> 791 us (0.989)
  local copies, waits for them, and re-layouts: 47.4 us -> 37.7 us
    all_to_all x2 -> x0, local copies, waits for them, and re-layouts: 12.9 us -> none  [per_device(): lax.all_to_all(slice_grad, 'seq', split_axis=1, concat_axis=2, tiled=True)]
    unnamed x11 -> x12, local copies, waits for them, and re-layouts: 23.3 us -> 24.2 us
where the time goes in v1:
time: 791 us; the launch traced here: 790 us
  waiting for transfers between devices  489 us (62%)
  blocking collectives  146 us (18%)
  matrix products  69.7 us (9%)
  local copies, waits for them, and re-layouts  37.7 us (5%)
  other arithmetic  28.3 us (4%)
  between operations  15.8 us (2%)
    reduce_scatter x1, waiting for transfers between devices, per_device(): lax.psum_scatter(jnp.einsum('bsd,dv->sbv', split_hidden, head_weight, pre...  259 us
    all_gather x1, waiting for transfers between devices, per_device(): all_grads = lax.all_gather(logit_grad, 'seq', axis=1, tiled=True)  127 us
    reduce_scatter x1, waiting for transfers between devices, per_device(): lax.psum_scatter(partial_grad, 'vocab', scatter_dimension=2, tiled=True)  95.2 us
    all_to_all x1, blocking collectives, per_device(): lax.all_to_all(jnp.stack(jnp.split(slice_grad, lax.axis_size('seq'), axis...  62.9 us
    all_to_all x1, blocking collectives, per_device(): lax.all_to_all(hidden, 'seq', split_axis=2, concat_axis=1, tiled=True)  35.6 us
    dot_general x1, matrix products, per_device(): jnp.einsum('bsv,dv->bsd', all_grads, head_weight, preferred_element_type=...  34.7 us
    dot_general x1, matrix products, per_device(): jnp.einsum('bsd,dv->sbv', split_hidden, head_weight, preferred_element_ty...  34.2 us
    unnamed x12, local copies, waits for them, and re-layouts  24.2 us
  transfers between devices with their start and end apart: 6, of which 6 were waited for; matrix products, arithmetic and copies ran while one was open for 3% of the time, Pallas kernels for 0%

profile of v1, /device:TPU:0, one launch (start us, length us, event | category | flops | bytes accessed | tf_op | source)
XLA Modules:
  0.0 790.0 jit_solution(3842077865711002288)
XLA Ops:
  7.2 0.0 reduce-scatter.3.cloned.1.call-start
  7.2 7.4 copy.22
  14.6 35.6 %all_to_all.23 = bf16[2,128,5120]{1,0,2:T(2,128)(2,1)S(1)} all-to-all(bf16[2,128,5120]{1,0,2:T(2,128)(2,1)} %copy.22), channel_id=1, replica_groups=mesh['seq'=4,'vocab'=8] {'seq'}, dimensions={2} | all-to-all | bytes 5242880 | tf_op jit(solution)/shard_map/all_to_all | solution.py:18
  50.2 4.6 copy.23
  54.9 34.2 %fusion.4 = f32[512,2,9728]{0,2,1:T(8,128)} fusion(bf16[2,512,1280]{2,1,0:T(8,128)(2,1)} %bitcast.49, bf16[1280,9728]{1,0:T(8,128)(2,1)} %param.8), kind=kOutput, calls=%fused_computation.4 | convolution fusion | flops 25501368320 | bytes 67371008 | tf_op jit(solution)/shard_map/bsd,dv->sbv/dot_general | solution.py:21
  89.1 0.0 reduce-scatter.3.cloned.1.call-update
  89.1 0.0 all-gather.2.cloned.1.call-start
  89.1 8.0 %copy.25 = bf16[2,128,9728]{1,2,0:T(8,128)(2,1)} copy(bf16[2,128,9728]{2,1,0:T(8,128)(2,1)} %param.9) | data formatting | bytes 9961472 | tf_op args[2]
  97.1 4.5 reduce_max.24
  101.6 258.7 %reduce-scatter.3.cloned.1.call-done = f32[128,2,9728]{0,2,1:T(8,128)} async-done(((f32[512,2,9728]{0,2,1:T(8,128)}), f32[128,2,9728]{0,2,1:T(8,128)}) %reduce-scatter.3.cloned.1.call-update) | async-done | bytes 9961488 | tf_op jit(solution)/shard_map/reduce_scatter | solution.py:20
  360.3 4.6 bitcast_reduce_fusion
  364.9 21.3 %all-reduce.1 = (f32[2,128]{1,0:T(2,128)S(1)}, f32[2,128]{1,0:T(2,128)S(1)}) all-reduce(f32[2,128]{1,0:T(2,128)S(1)} %bitcast_reduce_fusion, bf16[2,128]{1,0:T(2,128)(2,1)S(1)} %reduce_max.24), channel_id=1, replica_groups=mesh['seq'=4,'vocab'=8] {'vocab'}, use_global_device_ids=true, to_apply=%region_2.0 | all-reduce | flops 512 | bytes 3584 | tf_op jit(solution)/shard_map/pmax | solution.py:33
  386.2 0.0 copy-start
  386.2 0.0 copy-start.2
  386.3 0.0 copy-start.3
  386.3 0.0 copy-start.1
  386.3 7.6 fusion.8
  393.8 17.1 %all-reduce = (f32[2,128]{1,0:T(2,128)S(1)}, f32[2,128]{1,0:T(2,128)S(1)}, f32[2,128]{1,0:T(2,128)S(1)}) all-reduce(f32[2,128]{1,0:T(2,128)S(1)} %get-tuple-element.13, f32[2,128]{1,0:T(2,128)S(1)} %get-tuple-element.14, f32[2,128]{1,0:T(2,128)S(1)} %get-tuple-element.12), channel_id=1, replica_groups=mesh['seq'=4,'vocab'=8] {'vocab'}, use_global_device_ids=true, to_apply=%region_6.0 | all-reduce | flops 768 | bytes 6144 | tf_op jit(solution)/shard_map/psum | solution.py:35
  411.0 0.0 copy-done
  411.0 0.0 copy-done.2
  411.0 0.0 copy-done.3
  411.0 0.2 fusion.20
  411.2 1.3 collective-permute-start
  412.5 1.8 collective-permute-done
  414.2 1.3 collective-permute-start.1
  415.5 2.0 collective-permute-done.1
  417.6 1.3 collective-permute-start.2
  418.9 3.6 collective-permute-done.2
  422.4 0.8 select_reduce_fusion
  423.2 8.8 %all-reduce.2 = (f32[]{:T(128)}, f32[]{:T(128)}, f32[]{:T(128)}) all-reduce(f32[]{:T(128)} %get-tuple-element.16, f32[]{:T(128)} %get-tuple-element.17, f32[]{:T(128)} %get-tuple-element.15), channel_id=1, replica_groups=mesh['seq'=4,'vocab'=8] {'seq'}, use_global_device_ids=true, to_apply=%region_17.0 | all-reduce | flops 3 | bytes 24 | tf_op jit(solution)/shard_map/psum | solution.py:60
  434.0 0.6 select_divide_fusion
  434.6 0.0 copy-done.1
  434.6 9.3 %fusion.16 = bf16[2,128,9728]{1,2,0:T(8,128)(2,1)} fusion(f32[128,2,9728]{0,2,1:T(8,128)} %reduce-scatter.3.cloned.1.call-done, s32[2,128]{1,0:T(2,128)S(1)} %copy-done.1, f32[2,128]{1,0:T(2,128)S(1)} %get-tuple-element.31, f32[2,128]{1,0:T(2,128)S(1)} %get-tuple-element.26, s32[9728]{0:T(1024)S(1)} %iota_add_fusion), kind=kLoop, calls=%fused_computation.19 | loop fusion | flops 14942208 | bytes 14984192 | tf_op jit(solution)/shard_map/convert_element_type | solution.py:71
  444.0 0.0 all-gather.2.cloned.1.call-update
  444.0 0.0 reduce-scatter.5.cloned.1.call-start
  444.0 127.4 %all-gather.2.cloned.1.call-done = bf16[2,512,9728]{1,2,0:T(8,128)(2,1)} async-done(((bf16[2,128,9728]{1,2,0:T(8,128)(2,1)}), bf16[2,512,9728]{1,2,0:T(8,128)(2,1)}) %all-gather.2.cloned.1.call-update) | async-done | bytes 19922960 | tf_op jit(solution)/shard_map/all_gather | solution.py:72
  571.4 34.7 %fusion = f32[2,512,1280]{2,1,0:T(8,128)} fusion(bf16[2,512,9728]{1,2,0:T(8,128)(2,1)} %all-gather.2.cloned.1.call-done, bf16[1280,9728]{1,0:T(8,128)(2,1)} %param.8), kind=kOutput, calls=%fused_computation | convolution fusion | flops 25501368320 | bytes 50069504 | tf_op jit(solution)/shard_map/bsv,dv->bsd/dot_general | solution.py:73
  606.2 2.9 slice_bitcast_fusion.3
  609.1 0.4 pad_maximum_fusion
  609.5 62.9 %all_to_all.24 = f32[4,2,128,1280]{3,2,1,0:T(8,128)} all-to-all(f32[4,2,128,1280]{3,2,1,0:T(8,128)S(1)} %pad_maximum_fusion), channel_id=1, replica_groups=mesh['seq'=4,'vocab'=8] {'seq'}, dimensions={0} | all-to-all | bytes 10485760 | tf_op jit(solution)/shard_map/all_to_all | solution.py:77
  672.4 5.9 copy.27
  678.3 0.0 reduce-scatter.5.cloned.1.call-update
  678.3 7.9 %copy.28 = bf16[2,128,9728]{2,1,0:T(8,128)(2,1)} copy(bf16[2,128,9728]{1,2,0:T(8,128)(2,1)} %fusion.16) | data formatting | bytes 9961472
  686.2 95.2 %reduce-scatter.5.cloned.1.call-done = f32[2,128,640]{1,2,0:T(8,128)} async-done(((f32[2,128,5120]{1,2,0:T(8,128)}), f32[2,128,640]{1,2,0:T(8,128)}) %reduce-scatter.5.cloned.1.call-update) | async-done | bytes 655376 | tf_op jit(solution)/shard_map/reduce_scatter | solution.py:80
  781.5 1.1 convert_element_type.21
  782.6 0.9 copy.29
  (4 shorter events, 0.0 us)
Async XLA Ops:
  7.2 353.2 %reduce-scatter.3.cloned.1.call-start = ((), (), s32[]{:S(2)}) async-start(), calls=%async_computation.4 | async-start | bytes 49807360 | tf_op jit(solution)/shard_map/reduce_scatter | solution.py:20
  89.1 482.3 %all-gather.2.cloned.1.call-start = ((), (), s32[]{:S(2)}) async-start(), calls=%async_computation.5 | async-start | bytes 24903680 | tf_op jit(solution)/shard_map/all_gather | solution.py:72
  386.2 24.7 %copy-start = (s32[2,128]{1,0:T(2,128)S(1)}, s32[2,128]{1,0:T(2,128)}, u32[]{:S(2)}) copy-start(s32[2,128]{1,0:T(2,128)} %param.12) | copy-start | bytes 3076
  386.2 24.7 %copy-start.2 = (f32[2]{0:T(128)S(1)}, f32[2]{0:T(128)}, u32[]{:S(2)}) copy-start(f32[2]{0:T(128)} %param.13) | copy-start | bytes 28
  386.3 24.7 %copy-start.3 = (s32[2]{0:T(128)S(1)}, s32[2]{0:T(128)}, u32[]{:S(2)}) copy-start(s32[2]{0:T(128)} %param.11) | copy-start | bytes 28
  386.3 48.4 %copy-start.1 = (s32[2,128]{1,0:T(2,128)S(1)}, s32[2,128]{1,0:T(2,128)}, u32[]{:S(2)}) copy-start(s32[2,128]{1,0:T(2,128)} %param.10) | copy-start | bytes 3076
  411.2 3.0 collective-permute-start
  414.2 3.3 collective-permute-start.1
  417.6 4.9 collective-permute-start.2
  444.0 337.5 %reduce-scatter.5.cloned.1.call-start = ((), (), s32[]{:S(2)}) async-start(), calls=%async_computation.6 | async-start | bytes 5898240 | tf_op jit(solution)/shard_map/reduce_scatter | solution.py:80
Sparse Core Ops, SparseCore 0:
  89.2 271.0 reduce-scatter.2
  444.1 127.2 all-gather.1
  678.4 102.9 reduce-scatter.4
